TPU v7x, 128 devices: a whole 4x4x4 slice. The times are simulated.
128 devices in a mesh: seq: 4 (over y_hi, core), fsdp: 32 (over z, x, y_lo).
Axes of the slice: x: 4, y: 4 (y_hi: 2, y_lo: 2; y = y_hi * 2 + y_lo), z: 4, core: 2. Of those that a mesh axis runs over, the one named last changes fastest.
Arguments:
- hidden_in: bfloat16 [2048, 16384], P('seq', 'fsdp'), may hold values from -6 to 6
- gain_in: float32 [16384], P('fsdp'), may hold values from 0.25 to 1.75
- w_query: bfloat16 [16384, 4096], P('fsdp'), may hold values from -0.046875 to 0.046875
- query_scale: float32 [4096], replicated, may hold values from 0.5 to 2
- w_key: bfloat16 [16384, 256], P('fsdp'), may hold values from -0.046875 to 0.046875
- key_scale: float32 [256], replicated, may hold values from 0.5 to 2
- w_value: bfloat16 [16384, 256], P('fsdp'), may hold values from -0.046875 to 0.046875
- value_scale: float32 [256], replicated, may hold values from 0.5 to 2
- w_out: bfloat16 [4096, 16384], P(None, 'fsdp'), may hold values from -0.125 to 0.125
- out_scale: float32 [16384], P('fsdp'), may hold values from 0.5 to 2
- gain_mid: float32 [16384], P('fsdp'), may hold values from 0.25 to 1.75
- head_order: int32 [32], replicated, may hold values from 0 to 31, each once
Outputs:
- hessian: float32 [16384, 16384], P('fsdp', 'seq')
- residual_out: bfloat16 [2048, 16384], P('seq', 'fsdp')
All inputs are finite; a program needn't handle non-finite values.
Results may differ from a plain program's by a relative error of at most 0.009.
Values may be sent and summed in bfloat16 or wider, within the bound.
No kernel may reach another device: no remote copies, remote signals or barrier semaphores. Data moves between devices by JAX's collectives and lax.ppermute only.
A program may use at most 128 MiB of HBM per device.

v0:
```python
import jax
import jax.numpy as jnp
from jax import lax
from jax.sharding import PartitionSpec as P

D = 16384
HEAD = 128
GROUP = 16
KVW = 2
L = 256
KEEP = 16
epsilon = 1e-05


def sent_to_all(array, axis):
    copies = jnp.broadcast_to(array, (lax.axis_size(axis), *array.shape))
    return lax.all_to_all(copies, axis, split_axis=0, concat_axis=0, tiled=True)


def over_copies(array, axis):
    return sent_to_all(array, axis).sum(axis=0)


def in_order(pieces, dim):
    pieces = jnp.moveaxis(pieces, 0, dim)
    shape = pieces.shape
    return pieces.reshape(*shape[:dim], shape[dim] * shape[dim + 1], *shape[dim + 2 :])


def gather_directly(array, axis, dim):
    pieces = sent_to_all(array, axis)
    return in_order(pieces, dim)


def rotate(values_in, positions):
    half_size = values_in.shape[-1] // 2
    steps_idx = jnp.arange(half_size, dtype=jnp.float32)
    frequency = jnp.exp(-jnp.log(jnp.float32(500000.0)) * steps_idx * 2.0 / values_in.shape[-1])
    angles = positions.astype(jnp.float32)[:, None] * frequency[None, :]
    cosine = jnp.cos(angles)[:, None, :]
    sine = jnp.sin(angles)[:, None, :]
    first_half = values_in[..., :half_size]
    second_half = values_in[..., half_size:]
    return jnp.concatenate(
        [first_half * cosine - second_half * sine, second_half * cosine + first_half * sine],
        axis=-1,
    )


def shards(
    hidden_in,
    gain_in,
    w_query,
    query_scale,
    w_key,
    key_scale,
    w_value,
    value_scale,
    w_out,
    out_scale,
    gain_mid,
    head_order,
):
    group_tok = hidden_in.shape[0]
    shard_count = lax.axis_size("fsdp")
    seq_count = lax.axis_size("seq")
    row_count = group_tok // shard_count
    first_row = lax.axis_index("fsdp") * row_count
    kv_width = w_key.shape[1]
    hidden_f = hidden_in.astype(jnp.float32)
    square_sum = over_copies(jnp.sum(hidden_f * hidden_f, axis=1), "fsdp")
    inverse = lax.rsqrt(square_sum / D + epsilon)
    normed = (hidden_f * inverse[:, None] * gain_in[None, :]).astype(jnp.bfloat16)
    kept_heads = head_order[:KEEP]
    head_cols = (kept_heads[:, None] * HEAD + jnp.arange(HEAD, dtype=jnp.int32)[None, :]).reshape(
        -1
    )
    kv_weight = jnp.concatenate([w_key, w_value], axis=1)
    kv_scales = jnp.concatenate([key_scale, value_scale])
    my_positions = (first_row + jnp.arange(row_count, dtype=jnp.int32)) % L
    query_w = jnp.take(w_query, head_cols, axis=1)
    query_sc = jnp.take(query_scale, head_cols)
    query_width = query_w.shape[1]
    joint_w = jnp.concatenate([query_w, kv_weight], axis=1)
    summed = lax.psum_scatter(
        jnp.dot(normed, joint_w, preferred_element_type=jnp.float32),
        "fsdp",
        scatter_dimension=0,
        tiled=True,
    )
    query_rows = summed[:, :query_width] * query_sc[None, :]
    kv_summed = summed[:, query_width:]
    count_rows = kv_summed.shape[0]
    kv_scaled = kv_summed * kv_scales[None, :]
    key_rot = rotate(kv_scaled[:, :kv_width].reshape(count_rows, KVW, HEAD), my_positions).astype(
        jnp.bfloat16
    )
    value_part = kv_scaled[:, kv_width:].astype(jnp.bfloat16)
    kv_local = jnp.concatenate([key_rot.reshape(count_rows, kv_width), value_part], axis=1)
    kv_group = gather_directly(kv_local, "fsdp", 0)
    query_rot = rotate(query_rows.reshape(row_count, KEEP, HEAD), my_positions).astype(jnp.bfloat16)
    seq_start = first_row // L * L
    kv_seq = lax.dynamic_slice_in_dim(kv_group, seq_start, L, 0)
    key_seq = kv_seq[:, :kv_width].reshape(L, KVW, HEAD)
    value_seq = kv_seq[:, kv_width:].reshape(L, KVW, HEAD)
    select = ((kept_heads // GROUP)[:, None] == jnp.arange(KVW, dtype=jnp.int32)[None, :]).astype(
        jnp.bfloat16
    )
    key_heads = jnp.einsum(
        "lgd,hg->lhd", key_seq, select, preferred_element_type=jnp.float32
    ).astype(jnp.bfloat16)
    value_heads = jnp.einsum(
        "lgd,hg->lhd", value_seq, select, preferred_element_type=jnp.float32
    ).astype(jnp.bfloat16)
    scale_factor = 1.0 / jnp.sqrt(jnp.float32(HEAD))
    scores = (
        jnp.einsum("qhd,lhd->hql", query_rot, key_heads, preferred_element_type=jnp.float32)
        * scale_factor
    )
    causal = jnp.arange(L, dtype=jnp.int32)[None, :] <= my_positions[:, None]
    scores = jnp.where(causal[None], scores, -1e30)
    weights = jax.nn.softmax(scores, axis=-1).astype(jnp.bfloat16)
    attended = jnp.einsum("hql,lhd->qhd", weights, value_heads, preferred_element_type=jnp.float32)
    attended = attended.astype(jnp.bfloat16).reshape(row_count, KEEP * HEAD)
    out_w = jnp.take(w_out, head_cols, axis=0)
    mixed = (
        jnp.dot(gather_directly(attended, "fsdp", 0), out_w, preferred_element_type=jnp.float32)
        * out_scale[None, :]
    )
    residual_out = (hidden_f + mixed).astype(jnp.bfloat16)
    resid_f = residual_out.astype(jnp.float32)
    square_mid = over_copies(jnp.sum(resid_f * resid_f, axis=1), "fsdp")
    inverse_mid = lax.rsqrt(square_mid / D + epsilon)
    ffn_input = (resid_f * inverse_mid[:, None] * gain_mid[None, :]).astype(jnp.bfloat16)
    local_width = ffn_input.shape[1]
    rows_whole = gather_directly(ffn_input, "seq", 0)
    rows_whole = rows_whole.reshape(seq_count, shard_count, row_count, local_width)
    rows_whole = rows_whole.transpose(1, 0, 2, 3).reshape(seq_count * group_tok, local_width)
    relayed = lax.all_to_all(
        lax.all_to_all(ffn_input, "fsdp", split_axis=0, concat_axis=1, tiled=True),
        "seq",
        split_axis=1,
        concat_axis=0,
        tiled=True,
    )
    columns_whole = lax.all_gather(relayed, "fsdp", axis=0, tiled=True)
    tile_sum = lax.dot_general(
        rows_whole, columns_whole, (((0,), (0,)), ((), ())), preferred_element_type=jnp.float32
    )
    hessian = tile_sum / (seq_count * group_tok)
    return (hessian, residual_out)


def solution(mesh):
    return jax.shard_map(
        shards,
        mesh=mesh,
        in_specs=(
            P("seq", "fsdp"),
            P("fsdp"),
            P("fsdp", None),
            P(),
            P("fsdp", None),
            P(),
            P("fsdp", None),
            P(),
            P(None, "fsdp"),
            P("fsdp"),
            P("fsdp"),
            P(),
        ),
        out_specs=(P("fsdp", "seq"), P("seq", "fsdp")),
        check_vma=False,
    )
```

profile of v0, /device:TPU:24, one launch (start us, length us, event | category | flops | bytes accessed | tf_op | source)
XLA Modules:
  0.0 713.6 jit_solution(760770537415510053)
XLA Ops:
  7.2 1.2 fusion.27
  9.1 9.4 %all-to-all-start = ((f32[32,1,512]{2,1,0:T(1,128)}), f32[32,1,512]{2,1,0:T(1,128)S(1)}, u32[]{:S(2)}, u32[]{:S(2)}) async-start(f32[32,1,512]{2,1,0:T(1,128)} %broadcast_in_dim.48), calls=%async_computation | async-start | bytes 131072 | tf_op jit(solution)/shard_map/all_to_all | solution.py:17
  19.4 6.4 copy.61
  25.8 10.3 %gather_fusion = bf16[2048,512]{1,0:T(8,128)(2,1)S(1)} fusion(bf16[512,4096]{0,1:T(8,128)(2,1)} %copy.61, s32[2048]{0:T(1024)S(1)} %broadcast_clamp_fusion), kind=kCustom, calls=%fused_computation | custom fusion | bytes 4202496 | tf_op jit(solution)/shard_map/jit(_take)/gather | solution.py:81
  36.2 1.6 select_bitcast_fusion
  38.1 5.5 fusion.1
  43.7 11.8 %gather_fusion.1 = f32[2048]{0:T(1024)S(1)} fusion(f32[4096]{0:T(1024)S(1)} %copy-done, s32[2048]{0:T(1024)S(1)} %broadcast_clamp_fusion), kind=kCustom, calls=%fused_computation.1 | custom fusion | bytes 24576 | tf_op jit(solution)/shard_map/jit(_take)/gather | solution.py:82
  55.9 159.8 %reduce-scatter.2.cloned.1.call-done = f32[16,2560]{1,0:T(8,128)} async-done(((f32[512,2560]{1,0:T(8,128)}), f32[16,2560]{1,0:T(8,128)}) %reduce-scatter.2.cloned.1.call-update) | async-done | bytes 163856 | tf_op jit(solution)/shard_map/reduce_scatter | solution.py:85
  215.7 0.8 slice_multiply_fusion.1
  216.7 0.9 broadcast_in_dim.51
  217.6 7.7 %all-to-all-start.1 = ((bf16[32,16,512]{2,1,0:T(8,128)(2,1)}), bf16[32,16,512]{2,1,0:T(8,128)(2,1)S(1)}, u32[]{:S(2)}, u32[]{:S(2)}) async-start(bf16[32,16,512]{2,1,0:T(8,128)(2,1)} %broadcast_in_dim.51), calls=%async_computation.2 | async-start | bytes 1048576 | tf_op jit(solution)/shard_map/all_to_all | solution.py:17
  225.2 0.9 fusion.36
  226.4 11.5 %all-to-all-done.1 = bf16[32,16,512]{2,1,0:T(8,128)(2,1)S(1)} async-done(((bf16[32,16,512]{2,1,0:T(8,128)(2,1)}), bf16[32,16,512]{2,1,0:T(8,128)(2,1)S(1)}, u32[]{:S(2)}, u32[]{:S(2)}) %all-to-all-start.1) | async-done | bytes 524320 | tf_op jit(solution)/shard_map/all_to_all | solution.py:17
  240.0 1.6 broadcast_in_dim.84
  241.6 6.3 all-to-all-start.2
  247.9 10.3 %gather_fusion.2 = bf16[2048,512]{1,0:T(8,128)(2,1)S(1)} fusion(bf16[4096,512]{1,0:T(8,128)(2,1)} %param.20, s32[2048]{0:T(1024)S(1)} %broadcast_clamp_fusion), kind=kCustom, calls=%fused_computation.2 | custom fusion | bytes 4202496 | tf_op jit(solution)/shard_map/jit(_take)/gather | solution.py:125
  258.2 7.8 %all-to-all-done.2 = bf16[32,16,2048]{2,1,0:T(8,128)(2,1)} async-done(((bf16[32,16,2048]{2,1,0:T(8,128)(2,1)}), bf16[32,16,2048]{2,1,0:T(8,128)(2,1)}, u32[]{:S(2)}, u32[]{:S(2)}) %all-to-all-start.2) | async-done | bytes 2097184 | tf_op jit(solution)/shard_map/all_to_all | solution.py:17
  266.1 3.1 fusion.24
  269.2 13.7 %all_to_all.62 = f32[32,1,512]{2,1,0:T(1,128)S(1)} all-to-all(f32[32,1,512]{2,1,0:T(1,128)S(1)} %broadcast_in_dim.87), channel_id=1, replica_groups=mesh['seq'=4,'fsdp'=32] {'fsdp'}, dimensions={0} | all-to-all | bytes 131072 | tf_op jit(solution)/shard_map/all_to_all | solution.py:17
  283.2 13.9 %all_to_all.63 = bf16[32,16,512]{2,1,0:T(8,128)(2,1)S(1)} all-to-all(bf16[32,16,512]{2,1,0:T(8,128)(2,1)S(1)} %bitcast.49), channel_id=1, replica_groups=mesh['seq'=4,'fsdp'=32] {'fsdp'}, dimensions={0} | all-to-all | bytes 1048576 | tf_op jit(solution)/shard_map/all_to_all | solution.py:140
  298.1 11.9 %all_to_all.64 = bf16[16,4,4096]{2,0,1:T(8,128)(2,1)} all-to-all(bf16[16,4,4096]{2,0,1:T(8,128)(2,1)S(1)} %copy.72), channel_id=1, replica_groups=mesh['seq'=4,'fsdp'=32] {'seq'}, dimensions={1} | all-to-all | bytes 1048576 | tf_op jit(solution)/shard_map/all_to_all | solution.py:139
  310.2 74.8 %all_to_all.65 = bf16[4,512,512]{2,1,0:T(8,128)(2,1)S(1)} all-to-all(bf16[4,512,512]{2,1,0:T(8,128)(2,1)S(1)} %broadcast_in_dim.88), channel_id=1, replica_groups=mesh['seq'=4,'fsdp'=32] {'seq'}, dimensions={0} | all-to-all | bytes 4194304 | tf_op jit(solution)/shard_map/all_to_all | solution.py:17
  385.2 307.0 %all-gather.2.cloned.1.call-done = bf16[2048,4096]{1,0:T(8,128)(2,1)} async-done(((bf16[64,4096]{1,0:T(8,128)(2,1)}), bf16[2048,4096]{1,0:T(8,128)(2,1)}) %all-gather.2.cloned.1.call-update) | async-done | bytes 16777232 | tf_op jit(solution)/shard_map/all_gather | solution.py:146
  692.2 14.6 %convolution_multiply_fusion = f32[512,4096]{1,0:T(8,128)} fusion(bf16[2048,512]{1,0:T(8,128)(2,1)S(1)} %bitcast.50, bf16[2048,4096]{1,0:T(8,128)(2,1)} %all-gather.2.cloned.1.call-done), kind=kOutput, calls=%fused_computation.4 | convolution fusion | flops 8592031744 | bytes 27262976 | tf_op jit(solution)/shard_map/dot_general | solution.py:147
  (70 shorter events, 6.5 us)
Async XLA Ops:
  7.2 36.5 %copy-start = (f32[4096]{0:T(1024)S(1)}, f32[4096]{0:T(1024)}, u32[]{:S(2)}) copy-start(f32[4096]{0:T(1024)} %param.15) | copy-start | bytes 49156
  9.1 28.9 %all-to-all-start = ((f32[32,1,512]{2,1,0:T(1,128)}), f32[32,1,512]{2,1,0:T(1,128)S(1)}, u32[]{:S(2)}, u32[]{:S(2)}) async-start(f32[32,1,512]{2,1,0:T(1,128)} %broadcast_in_dim.48), calls=%async_computation | async-start | bytes 131072 | tf_op jit(solution)/shard_map/all_to_all | solution.py:17
  18.5 197.2 %reduce-scatter.2.cloned.1.call-start = ((), (), s32[]{:S(2)}) async-start(), calls=%async_computation.8 | async-start | bytes 5406720 | tf_op jit(solution)/shard_map/reduce_scatter | solution.py:85
  36.1 1.6 copy-start.4
  36.1 1.7 copy-start.5
  36.1 2.0 copy-start.2
  36.1 2.0 copy-start.9
  43.7 11.9 %copy-start.7 = (f32[256]{0:T(256)S(1)}, f32[256]{0:T(256)}, u32[]{:S(2)}) copy-start(f32[256]{0:T(256)} %param.19) | copy-start | bytes 3076
  43.7 11.9 %copy-start.8 = (f32[256]{0:T(256)S(1)}, f32[256]{0:T(256)}, u32[]{:S(2)}) copy-start(f32[256]{0:T(256)} %param.17) | copy-start | bytes 3076
  217.6 20.3 %all-to-all-start.1 = ((bf16[32,16,512]{2,1,0:T(8,128)(2,1)}), bf16[32,16,512]{2,1,0:T(8,128)(2,1)S(1)}, u32[]{:S(2)}, u32[]{:S(2)}) async-start(bf16[32,16,512]{2,1,0:T(8,128)(2,1)} %broadcast_in_dim.51), calls=%async_computation.2 | async-start | bytes 1048576 | tf_op jit(solution)/shard_map/all_to_all | solution.py:17
  241.6 24.5 %all-to-all-start.2 = ((bf16[32,16,2048]{2,1,0:T(8,128)(2,1)}), bf16[32,16,2048]{2,1,0:T(8,128)(2,1)}, u32[]{:S(2)}, u32[]{:S(2)}) async-start(bf16[32,16,2048]{2,1,0:T(8,128)(2,1)} %broadcast_in_dim.84), calls=%async_computation.3 | async-start | bytes 4194304 | tf_op jit(solution)/shard_map/all_to_all | solution.py:17
  247.9 18.2 %copy-start.10 = (f32[512]{0:T(512)S(1)}, f32[512]{0:T(512)}, u32[]{:S(2)}) copy-start(f32[512]{0:T(512)} %param.21) | copy-start | bytes 6148
  247.9 444.4 %all-gather.2.cloned.1.call-start = ((), (), s32[]{:S(2)}) async-start(), calls=%async_computation.9 | async-start | bytes 17301504 | tf_op jit(solution)/shard_map/all_gather | solution.py:146
  266.1 16.9 %copy-start.6 = (f32[512]{0:T(512)S(1)}, f32[512]{0:T(512)}, u32[]{:S(2)}) copy-start(f32[512]{0:T(512)} %param.22) | copy-start | bytes 6148
  269.1 28.7 %copy-start.3 = (bf16[512,512]{1,0:T(8,128)(2,1)}, bf16[512,512]{1,0:T(8,128)(2,1)S(1)}, u32[]{:S(2)}) copy-start(bf16[512,512]{1,0:T(8,128)(2,1)S(1)} %get-tuple-element.17) | copy-start | bytes 1572868
  692.2 14.6 %copy-start.1 = (f32[4096]{0:T(1024)S(1)}, f32[4096]{0:T(1024)}, u32[]{:S(2)}) copy-start(f32[4096]{0:T(1024)} %param.15) | copy-start | bytes 49156
Sparse Core Ops, SparseCore 0:
  43.8 171.8 reduce-scatter.1
  310.1 382.0 all-gather.1
where the time goes:
time: 715 us; the launch traced here: 714 us
  waiting for transfers between devices  486 us (68%)
  blocking collectives  114 us (16%)
  local copies, waits for them, and re-layouts  43.9 us (6%)
  matrix products  25.2 us (4%)
  starting transfers between devices  23.4 us (3%)
  between operations  14.4 us (2%)
    all_gather x1, waiting for transfers between devices, shards(): columns_whole = lax.all_gather(relayed, 'fsdp', axis=0, tiled=True)  307 us
    reduce_scatter x1, waiting for transfers between devices, shards(): lax.psum_scatter(jnp.dot(normed, joint_w, preferred_element_type=jnp.floa...  160 us
    all_to_all x2, blocking collectives, sent_to_all(): return lax.all_to_all(copies, axis, split_axis=0, concat_axis=0, tiled=True)  88.6 us
    all_to_all x3, starting transfers between devices, sent_to_all(): return lax.all_to_all(copies, axis, split_axis=0, concat_axis=0, tiled=True)  23.4 us
    all_to_all x3, waiting for transfers between devices, sent_to_all(): return lax.all_to_all(copies, axis, split_axis=0, concat_axis=0, tiled=True)  19.3 us
    dot_general x1, matrix products, shards(): lax.dot_general(rows_whole, columns_whole, (((0,), (0,)), ((), ())), pref...  14.6 us
  transfers between devices with their start and end apart: 5, of which 4 were waited for; matrix products, arithmetic and copies ran while one was open for 6% of the time, Pallas kernels for 0%

commit v1 on v0

--- a/solution.py
+++ b/solution.py
@@ -143,7 +143,8 @@
         concat_axis=0,
         tiled=True,
     )
-    columns_whole = lax.all_gather(relayed, "fsdp", axis=0, tiled=True)
+    repeated = jnp.stack([relayed] * lax.axis_size("fsdp"))
+    columns_whole = jnp.concatenate(lax.all_to_all(repeated, "fsdp", 0, 0), axis=0)
     tile_sum = lax.dot_general(
         rows_whole, columns_whole, (((0,), (0,)), ((), ())), preferred_element_type=jnp.float32
     )

time: 715 us -> 660 us (0.923)
  blocking collectives: 114 us -> 69.1 us
  waiting for transfers between devices: 486 us -> 461 us
  local copies, waits for them, and re-layouts: 43.9 us -> 51.2 us
    all_gather x1 -> x0, waiting for transfers between devices: 307 us -> none  [shards(): columns_whole = lax.all_gather(relayed, 'fsdp', axis=0, tiled=True)]
    all_to_all x0 -> x1, waiting for transfers between devices: none -> 281 us  [shards(): lax.all_to_all(repeated, 'fsdp', 0, 0)]
    all_to_all x2, blocking collectives: 88.6 us -> 43.4 us  [sent_to_all(): return lax.all_to_all(copies, axis, split_axis=0, concat_axis=0, tiled=True)]
  transfers between devices with their start and end apart: 5 -> 5, of which waited for: 4 -> 4; matrix products, arithmetic and copies ran while one was open for 6% -> 7% of each run, Pallas kernels for 0% -> 0%
where the time goes in v1:
time: 660 us; the launch traced here: 657 us
  waiting for transfers between devices  461 us (70%)
  blocking collectives  69.1 us (10%)
  local copies, waits for them, and re-layouts  51.2 us (8%)
  starting transfers between devices  29.8 us (5%)
  matrix products  25.7 us (4%)
  between operations  14.4 us (2%)
    all_to_all x1, waiting for transfers between devices, shards(): lax.all_to_all(repeated, 'fsdp', 0, 0)  281 us
    reduce_scatter x1, waiting for transfers between devices, shards(): lax.psum_scatter(jnp.dot(normed, joint_w, preferred_element_type=jnp.floa...  160 us
    all_to_all x2, blocking collectives, sent_to_all(): return lax.all_to_all(copies, axis, split_axis=0, concat_axis=0, tiled=True)  43.4 us
    all_to_all x3, starting transfers between devices, sent_to_all(): return lax.all_to_all(copies, axis, split_axis=0, concat_axis=0, tiled=True)  23.2 us
    all_to_all x3, waiting for transfers between devices, sent_to_all(): return lax.all_to_all(copies, axis, split_axis=0, concat_axis=0, tiled=True)  19.7 us
    dot_general x1, matrix products, shards(): lax.dot_general(rows_whole, columns_whole, (((0,), (0,)), ((), ())), pref...  15.2 us
    all_to_all x1, blocking collectives, shards(): lax.all_to_all(ffn_input, 'fsdp', split_axis=0, concat_axis=1, tiled=True)  13.9 us
  transfers between devices with their start and end apart: 5, of which 4 were waited for; matrix products, arithmetic and copies ran while one was open for 7% of the time, Pallas kernels for 0%

profile of v1, /device:TPU:24, one launch (start us, length us, event | category | flops | bytes accessed | tf_op | source)
XLA Modules:
  0.0 657.2 jit_solution(4919645649832026758)
XLA Ops:
  7.2 1.2 fusion.27
  9.1 9.4 %all-to-all-start = ((f32[32,1,512]{2,1,0:T(1,128)}), f32[32,1,512]{2,1,0:T(1,128)S(1)}, u32[]{:S(2)}, u32[]{:S(2)}) async-start(f32[32,1,512]{2,1,0:T(1,128)} %broadcast_in_dim.48), calls=%async_computation | async-start | bytes 131072 | tf_op jit(solution)/shard_map/all_to_all | solution.py:17
  19.4 6.4 copy.61
  25.8 10.3 %gather_fusion = bf16[2048,512]{1,0:T(8,128)(2,1)S(1)} fusion(bf16[512,4096]{0,1:T(8,128)(2,1)} %copy.61, s32[2048]{0:T(1024)S(1)} %broadcast_clamp_fusion), kind=kCustom, calls=%fused_computation | custom fusion | bytes 4202496 | tf_op jit(solution)/shard_map/jit(_take)/gather | solution.py:81
  36.1 1.6 select_bitcast_fusion
  38.1 5.5 fusion.1
  43.7 11.8 %gather_fusion.1 = f32[2048]{0:T(1024)S(1)} fusion(f32[4096]{0:T(1024)S(1)} %copy-done, s32[2048]{0:T(1024)S(1)} %broadcast_clamp_fusion), kind=kCustom, calls=%fused_computation.1 | custom fusion | bytes 24576 | tf_op jit(solution)/shard_map/jit(_take)/gather | solution.py:82
  55.9 160.1 %reduce-scatter.2.cloned.1.call-done = f32[16,2560]{1,0:T(8,128)} async-done(((f32[512,2560]{1,0:T(8,128)}), f32[16,2560]{1,0:T(8,128)}) %reduce-scatter.2.cloned.1.call-update) | async-done | bytes 163856 | tf_op jit(solution)/shard_map/reduce_scatter | solution.py:85
  217.8 7.7 %all-to-all-start.1 = ((bf16[32,16,512]{2,1,0:T(8,128)(2,1)}), bf16[32,16,512]{2,1,0:T(8,128)(2,1)S(1)}, u32[]{:S(2)}, u32[]{:S(2)}) async-start(bf16[32,16,512]{2,1,0:T(8,128)(2,1)} %broadcast_in_dim.51), calls=%async_computation.2 | async-start | bytes 1048576 | tf_op jit(solution)/shard_map/all_to_all | solution.py:17
  226.6 11.9 %all-to-all-done.1 = bf16[32,16,512]{2,1,0:T(8,128)(2,1)S(1)} async-done(((bf16[32,16,512]{2,1,0:T(8,128)(2,1)}), bf16[32,16,512]{2,1,0:T(8,128)(2,1)S(1)}, u32[]{:S(2)}, u32[]{:S(2)}) %all-to-all-start.1) | async-done | bytes 524320 | tf_op jit(solution)/shard_map/all_to_all | solution.py:17
  240.6 1.6 broadcast_in_dim.84
  242.2 6.2 all-to-all-start.2
  248.4 10.3 %gather_fusion.2 = bf16[2048,512]{1,0:T(8,128)(2,1)S(1)} fusion(bf16[4096,512]{1,0:T(8,128)(2,1)} %param.20, s32[2048]{0:T(1024)S(1)} %broadcast_clamp_fusion), kind=kCustom, calls=%fused_computation.2 | custom fusion | bytes 4202496 | tf_op jit(solution)/shard_map/jit(_take)/gather | solution.py:125
  258.7 7.9 %all-to-all-done.2 = bf16[32,16,2048]{2,1,0:T(8,128)(2,1)} async-done(((bf16[32,16,2048]{2,1,0:T(8,128)(2,1)}), bf16[32,16,2048]{2,1,0:T(8,128)(2,1)}, u32[]{:S(2)}, u32[]{:S(2)}) %all-to-all-start.2) | async-done | bytes 2097184 | tf_op jit(solution)/shard_map/all_to_all | solution.py:17
  266.6 3.1 fusion.24
  269.7 13.8 %all_to_all.64 = f32[32,1,512]{2,1,0:T(1,128)S(1)} all-to-all(f32[32,1,512]{2,1,0:T(1,128)S(1)} %broadcast_in_dim.87), channel_id=1, replica_groups=mesh['seq'=4,'fsdp'=32] {'fsdp'}, dimensions={0} | all-to-all | bytes 131072 | tf_op jit(solution)/shard_map/all_to_all | solution.py:17
  283.7 13.9 %all_to_all.65 = bf16[32,16,512]{2,1,0:T(8,128)(2,1)S(1)} all-to-all(bf16[32,16,512]{2,1,0:T(8,128)(2,1)S(1)} %bitcast.50), channel_id=1, replica_groups=mesh['seq'=4,'fsdp'=32] {'fsdp'}, dimensions={0} | all-to-all | bytes 1048576 | tf_op jit(solution)/shard_map/all_to_all | solution.py:140
  298.6 11.8 %all_to_all.66 = bf16[16,4,4096]{2,0,1:T(8,128)(2,1)S(1)} all-to-all(bf16[16,4,4096]{2,0,1:T(8,128)(2,1)S(1)} %copy.72), channel_id=1, replica_groups=mesh['seq'=4,'fsdp'=32] {'seq'}, dimensions={1} | all-to-all | bytes 1048576 | tf_op jit(solution)/shard_map/all_to_all | solution.py:139
  310.6 29.6 %all_to_all.67 = bf16[4,512,512]{2,1,0:T(8,128)(2,1)S(1)} all-to-all(bf16[4,512,512]{2,1,0:T(8,128)(2,1)S(1)} %broadcast_in_dim.88), channel_id=1, replica_groups=mesh['seq'=4,'fsdp'=32] {'seq'}, dimensions={0} | all-to-all | bytes 4194304 | tf_op jit(solution)/shard_map/all_to_all | solution.py:17
  340.2 5.9 stack.5
  346.1 6.5 all-to-all-start.7
  352.6 1.6 copy.70
  354.2 280.9 %all-to-all-done.7 = bf16[32,64,4096]{2,1,0:T(8,128)(2,1)} async-done(((bf16[32,64,4096]{2,1,0:T(8,128)(2,1)}), bf16[32,64,4096]{2,1,0:T(8,128)(2,1)}, u32[]{:S(2)}, u32[]{:S(2)}) %all-to-all-start.7) | async-done | bytes 16777248 | tf_op jit(solution)/shard_map/all_to_all | solution.py:147
  635.2 15.2 %convolution_multiply_fusion = f32[512,4096]{1,0:T(8,128)} fusion(bf16[2048,512]{1,0:T(8,128)(2,1)} %bitcast.52, bf16[2048,4096]{1,0:T(8,128)(2,1)} %bitcast.17), kind=kOutput, calls=%fused_computation.4 | convolution fusion | flops 8592031744 | bytes 27262976 | tf_op jit(solution)/shard_map/dot_general | solution.py:148
  (70 shorter events, 8.8 us)
Async XLA Ops:
  7.2 36.5 %copy-start = (f32[4096]{0:T(1024)S(1)}, f32[4096]{0:T(1024)}, u32[]{:S(2)}) copy-start(f32[4096]{0:T(1024)} %param.15) | copy-start | bytes 49156
  9.1 28.9 %all-to-all-start = ((f32[32,1,512]{2,1,0:T(1,128)}), f32[32,1,512]{2,1,0:T(1,128)S(1)}, u32[]{:S(2)}, u32[]{:S(2)}) async-start(f32[32,1,512]{2,1,0:T(1,128)} %broadcast_in_dim.48), calls=%async_computation | async-start | bytes 131072 | tf_op jit(solution)/shard_map/all_to_all | solution.py:17
  18.5 197.5 %reduce-scatter.2.cloned.1.call-start = ((), (), s32[]{:S(2)}) async-start(), calls=%async_computation.9 | async-start | bytes 5406720 | tf_op jit(solution)/shard_map/reduce_scatter | solution.py:85
  36.1 1.6 copy-start.4
  36.1 1.8 copy-start.5
  36.1 2.0 copy-start.2
  36.1 2.0 copy-start.9
  43.7 11.9 %copy-start.7 = (f32[256]{0:T(256)S(1)}, f32[256]{0:T(256)}, u32[]{:S(2)}) copy-start(f32[256]{0:T(256)} %param.19) | copy-start | bytes 3076
  43.7 11.9 %copy-start.8 = (f32[256]{0:T(256)S(1)}, f32[256]{0:T(256)}, u32[]{:S(2)}) copy-start(f32[256]{0:T(256)} %param.17) | copy-start | bytes 3076
  217.8 20.7 %all-to-all-start.1 = ((bf16[32,16,512]{2,1,0:T(8,128)(2,1)}), bf16[32,16,512]{2,1,0:T(8,128)(2,1)S(1)}, u32[]{:S(2)}, u32[]{:S(2)}) async-start(bf16[32,16,512]{2,1,0:T(8,128)(2,1)} %broadcast_in_dim.51), calls=%async_computation.2 | async-start | bytes 1048576 | tf_op jit(solution)/shard_map/all_to_all | solution.py:17
  242.2 24.4 %all-to-all-start.2 = ((bf16[32,16,2048]{2,1,0:T(8,128)(2,1)}), bf16[32,16,2048]{2,1,0:T(8,128)(2,1)}, u32[]{:S(2)}, u32[]{:S(2)}) async-start(bf16[32,16,2048]{2,1,0:T(8,128)(2,1)} %broadcast_in_dim.84), calls=%async_computation.3 | async-start | bytes 4194304 | tf_op jit(solution)/shard_map/all_to_all | solution.py:17
  248.4 18.2 %copy-start.10 = (f32[512]{0:T(512)S(1)}, f32[512]{0:T(512)}, u32[]{:S(2)}) copy-start(f32[512]{0:T(512)} %param.21) | copy-start | bytes 6148
  266.6 16.9 %copy-start.6 = (f32[512]{0:T(512)S(1)}, f32[512]{0:T(512)}, u32[]{:S(2)}) copy-start(f32[512]{0:T(512)} %param.22) | copy-start | bytes 6148
  269.6 28.7 %copy-start.3 = (bf16[512,512]{1,0:T(8,128)(2,1)}, bf16[512,512]{1,0:T(8,128)(2,1)S(1)}, u32[]{:S(2)}) copy-start(bf16[512,512]{1,0:T(8,128)(2,1)S(1)} %get-tuple-element.17) | copy-start | bytes 1572868
  346.1 289.0 %all-to-all-start.7 = ((bf16[32,64,4096]{2,1,0:T(8,128)(2,1)}), bf16[32,64,4096]{2,1,0:T(8,128)(2,1)}, u32[]{:S(2)}, u32[]{:S(2)}) async-start(bf16[32,64,4096]{2,1,0:T(8,128)(2,1)} %stack.5), calls=%async_computation.8 | async-start | bytes 33554432 | tf_op jit(solution)/shard_map/all_to_all | solution.py:147
  635.2 15.2 %copy-start.1 = (f32[4096]{0:T(1024)S(1)}, f32[4096]{0:T(1024)}, u32[]{:S(2)}) copy-start(f32[4096]{0:T(1024)} %param.15) | copy-start | bytes 49156
Sparse Core Ops, SparseCore 0:
  43.8 172.1 reduce-scatter.1
